TPU v7x, 256 devices: a whole 4x4x8 slice. The times are simulated.
256 devices in a mesh: ctx: 8 (over y, z_lo), exp: 16 (over z_hi, x), rep: 2 (over core).
Axes of the slice: x: 4, y: 4, z: 8 (z_hi: 4, z_lo: 2; z = z_hi * 2 + z_lo), core: 2. Of those that a mesh axis runs over, the one named last changes fastest.
Arguments:
- hidden_in: bfloat16 [8192, 4096], P(('rep', 'ctx', 'exp')), parts along dimension 0, may hold values from -6 to 6
- queries: bfloat16 [8192, 8192], P(('rep', 'ctx'), 'exp'), parts along dimension 0, may hold values from -64 to 64
- keys: bfloat16 [8192, 512], P(('rep', 'ctx')), parts along dimension 0, may hold values from -8 to 8
- values: bfloat16 [8192, 512], P(('rep', 'ctx')), parts along dimension 0, may hold values from -6 to 6
- out_proj: bfloat16 [8192, 4096], P('exp'), may hold values from -0.0625 to 0.0625
- norm_gain: float32 [4096], replicated, may hold values from 0.1 to 1.9
- expert_ids: int32 [8192, 8], P(('rep', 'ctx', 'exp')), parts along dimension 0, may hold values from 0 to 127, all different within a row; in each aligned block of 32 rows (0 to 31, 32 to 63, ...) at most 2 rows name the same one
- gate_fixed: int32 [8192, 8], P(('rep', 'ctx', 'exp')), parts along dimension 0, may hold values from 1 to 4096
- live_counts: int32 [256], P(('rep', 'ctx', 'exp')), parts along dimension 0, may hold values from 16 to 32, as said below
- gate_proj: bfloat16 [16, 4096, 1536], P('exp', None, 'ctx'), may hold values from -0.09375 to 0.09375
- up_proj: bfloat16 [16, 4096, 1536], P('exp', None, 'ctx'), may hold values from -0.09375 to 0.09375
- down_proj: bfloat16 [16, 1536, 4096], P('exp', 'ctx'), may hold values from -0.4375 to 0.4375
Outputs:
- mixed: bfloat16 [8192, 4096], P(('rep', 'ctx', 'exp')), parts along dimension 0
- expert_sum: bfloat16 [8192, 4096], P(('rep', 'ctx', 'exp')), parts along dimension 0
There are 2 independent parts, one for each index of `rep`. A program takes and returns all parts, laid end to end along the dimension named above; an argument that names none is the same for every part. Nothing has to cross between parts.
Inputs may be any that keep to these rules, and one draw needn't show every extreme that they name: `expert_ids`: each row names 8 different experts; among the 32 rows of one device no expert is named by more than 2 rows. `live_counts`: some device has all of its rows live.
All inputs are finite; a program needn't handle non-finite values.
Results may differ from a plain program's by a relative error of at most 0.023.
Values may be sent and summed in bfloat16 or wider, within the bound.
No kernel may reach another device: no remote copies, remote signals or barrier semaphores. Data moves between devices by JAX's collectives and lax.ppermute only.
A program may use at most 64 MiB of HBM per device.

v0:
```python
import jax
import jax.numpy as jnp
from jax import lax
from jax.sharding import PartitionSpec as P

D = 4096
HEADS = 64
KV_HEADS = 4
HEAD_DIM = 128
TOPK = 8
CAP = 2


def on_device(
    hidden_in,
    queries,
    keys,
    values,
    out_proj,
    norm_gain,
    expert_ids,
    gate_fixed,
    live_counts,
    gate_proj,
    up_proj,
    down_proj,
):
    n_ctx = lax.axis_size("ctx")
    n_exp = lax.axis_size("exp")
    seq_rows = queries.shape[0]
    local_heads = queries.shape[1] // HEAD_DIM
    group = HEADS // KV_HEADS
    kv_index = lax.axis_index("exp") * local_heads // group
    key_head = lax.dynamic_slice_in_dim(keys, kv_index * HEAD_DIM, HEAD_DIM, 1)
    value_head = lax.dynamic_slice_in_dim(values, kv_index * HEAD_DIM, HEAD_DIM, 1)
    query_heads = queries.reshape(seq_rows, local_heads, HEAD_DIM).transpose(1, 0, 2)
    query_pos = lax.axis_index("ctx") * seq_rows + jnp.arange(seq_rows, dtype=jnp.int32)
    scale = HEAD_DIM ** (-0.5)

    def update(carry, key_block, value_block, first):
        running, total, accum = carry
        scores = (
            jnp.einsum("hqd,kd->hqk", query_heads, key_block, preferred_element_type=jnp.float32)
            * scale
        )
        key_pos = first + jnp.arange(seq_rows, dtype=jnp.int32)
        visible = (key_pos[None, :] <= query_pos[:, None])[None]
        scores = jnp.where(visible, scores, -1e30)
        newest = jnp.maximum(running, jnp.max(scores, axis=2))
        weights = jnp.where(visible, jnp.exp(scores - newest[..., None]), 0.0)
        factor = jnp.exp(running - newest)
        total = total * factor + jnp.sum(weights, axis=2)
        accum = accum * factor[..., None] + jnp.einsum(
            "hqk,kd->hqd",
            weights.astype(jnp.bfloat16),
            value_block,
            preferred_element_type=jnp.float32,
        )
        return (newest, total, accum)

    start_state = (
        jnp.full((local_heads, seq_rows), -1e30, jnp.float32),
        jnp.zeros((local_heads, seq_rows), jnp.float32),
        jnp.zeros((local_heads, seq_rows, HEAD_DIM), jnp.float32),
    )
    carry = start_state
    key_piece = lax.all_gather(key_head, "ctx", axis=0, tiled=True)
    value_piece = lax.all_gather(value_head, "ctx", axis=0, tiled=True)
    blocks = key_piece.shape[0] // seq_rows
    key_blocks = key_piece.reshape(blocks, seq_rows, HEAD_DIM)
    value_blocks = value_piece.reshape(blocks, seq_rows, HEAD_DIM)
    firsts = jnp.arange(blocks, dtype=jnp.int32) * seq_rows

    def step(state, inputs):
        key_block, value_block, first = inputs
        state = update(state, key_block, value_block, first)
        return (state, None)

    carry, _ = lax.scan(step, carry, (key_blocks, value_blocks, firsts))
    running, total, accum = carry
    attended = (
        (accum / total[..., None])
        .astype(jnp.bfloat16)
        .transpose(1, 0, 2)
        .reshape(seq_rows, local_heads * HEAD_DIM)
    )
    token_rows = hidden_in.shape[0]
    attn_out = lax.psum_scatter(
        jnp.dot(attended, out_proj, preferred_element_type=jnp.float32).astype(jnp.bfloat16),
        "exp",
        scatter_dimension=0,
        tiled=True,
    ).astype(jnp.float32)
    residual = hidden_in.astype(jnp.float32) + attn_out
    mixed = residual.astype(jnp.bfloat16)
    norm_scale = lax.rsqrt(jnp.mean(residual * residual, axis=1, keepdims=True) + 1e-06)
    normed = (residual * norm_scale * norm_gain).astype(jnp.bfloat16)
    slot_count = n_exp * CAP
    live = jnp.arange(token_rows, dtype=jnp.int32) < live_counts[0]
    active = (expert_ids < n_exp) & live[:, None]
    onehot = (
        (expert_ids[..., None] == jnp.arange(n_exp, dtype=jnp.int32)) & active[..., None]
    ).astype(jnp.int32)
    onehot = onehot.reshape(token_rows * TOPK, n_exp)
    earlier = jnp.cumsum(onehot, axis=0) - onehot
    rank = jnp.sum(earlier * onehot, axis=1).reshape(token_rows, TOPK)
    slot = jnp.where(active, expert_ids * CAP + rank, -1)
    pair_hit = slot[..., None] == jnp.arange(slot_count, dtype=jnp.int32)
    dispatch = jnp.any(pair_hit, axis=1).astype(jnp.bfloat16)
    send = jnp.einsum("rs,rd->sd", dispatch, normed, preferred_element_type=jnp.float32).astype(
        jnp.bfloat16
    )
    send = send.reshape(n_exp, CAP, D)
    route_weights = gate_fixed.astype(jnp.float32) / 4096.0
    combine = jnp.sum(pair_hit.astype(jnp.float32) * route_weights[..., None], axis=1)
    copies = jnp.broadcast_to(send[None], (n_ctx, n_exp, CAP, D)).reshape(n_ctx * n_exp, CAP, D)
    rows3 = lax.all_to_all(copies, ("ctx", "exp"), split_axis=0, concat_axis=0, tiled=True)
    flat_rows = rows3.reshape(-1, D)
    gate_part = jnp.dot(flat_rows, gate_proj[0], preferred_element_type=jnp.float32)
    up_part = jnp.dot(flat_rows, up_proj[0], preferred_element_type=jnp.float32)
    hidden = (jax.nn.silu(gate_part) * up_part).astype(jnp.bfloat16)
    partial_value = jnp.dot(hidden, down_proj[0], preferred_element_type=jnp.float32)
    partial_value = partial_value.reshape(rows3.shape[0], rows3.shape[1], D).astype(jnp.bfloat16)
    returned = lax.all_to_all(
        partial_value, ("ctx", "exp"), split_axis=0, concat_axis=0, tiled=True
    )
    expert_out = (
        returned.astype(jnp.float32).reshape(n_ctx, slot_count, D).sum(axis=0).astype(jnp.bfloat16)
    )
    expert_sum = jnp.dot(combine, expert_out.astype(jnp.float32), precision=lax.Precision.HIGHEST)
    return (mixed, expert_sum.astype(jnp.bfloat16))


def solution(mesh):
    in_specs = (
        P(("rep", "ctx", "exp"), None),
        P(("rep", "ctx"), "exp"),
        P(("rep", "ctx"), None),
        P(("rep", "ctx"), None),
        P("exp", None),
        P(),
        P(("rep", "ctx", "exp"), None),
        P(("rep", "ctx", "exp"), None),
        P(("rep", "ctx", "exp")),
        P("exp", None, "ctx"),
        P("exp", None, "ctx"),
        P("exp", "ctx", None),
    )
    out_specs = (P(("rep", "ctx", "exp"), None), P(("rep", "ctx", "exp"), None))
    return jax.shard_map(
        on_device, mesh=mesh, in_specs=in_specs, out_specs=out_specs, check_vma=False
    )
```

profile of v0, /device:TPU:64, one launch (start us, length us, event | category | flops | bytes accessed | tf_op | source)
XLA Modules:
  0.0 457.7 jit_solution(1210172698889403102)
XLA Ops:
  7.2 1.7 constant_dynamic-slice_fusion.1
  9.0 1.6 constant_dynamic-slice_fusion
  10.7 1.3 copy.45
  12.2 43.5 %all-gather.3.cloned.1.call-done = bf16[4096,128]{1,0:T(8,128)(2,1)} async-done(((bf16[512,128]{1,0:T(8,128)(2,1)}), bf16[4096,128]{1,0:T(8,128)(2,1)}) %all-gather.3.cloned.1.call-update) | async-done | bytes 1048592 | tf_op jit(solution)/shard_map/all_gather | solution.py:67
  55.7 44.4 %all-gather.5.cloned.1.call-done = bf16[4096,128]{1,0:T(8,128)(2,1)} async-done(((bf16[512,128]{1,0:T(8,128)(2,1)}), bf16[4096,128]{1,0:T(8,128)(2,1)}) %all-gather.5.cloned.1.call-update) | async-done | bytes 1048592 | tf_op jit(solution)/shard_map/all_gather | solution.py:68
  100.1 100.9 %while.15 = (s32[]{:T(128)}, f32[4,512]{1,0:T(4,128)S(1)}, f32[4,512]{1,0:T(4,128)S(1)}, f32[4,512,128]{2,1,0:T(8,128)}, s32[8]{0:T(128)S(1)}, /*index=5*/bf16[8...) while((s32[]{:T(128)}, f32[4,512]{1,0:T(4,128)S(1)}, ...), condition=%wide.region_3.4_spmd.clone, body=%wide.region_0.3_spmd.clone.sunk | while | flops 551562240 | bytes 41821408 | solution.py:79
  100.6 0.6 iota_add_fusion.3
  101.5 3.8 fusion.62
  105.3 3.4 fusion.63
  108.8 2.9 fusion.65
  111.7 1.0 copy-done.4
  113.2 0.6 iota_add_fusion.3
  114.1 3.8 fusion.62
  117.9 3.4 fusion.63
  121.4 2.9 fusion.65
  124.3 1.0 copy-done.4
  125.9 0.6 iota_add_fusion.3
  126.7 3.8 fusion.62
  130.5 3.4 fusion.63
  134.0 2.9 fusion.65
  136.9 1.0 copy-done.4
  138.5 0.6 iota_add_fusion.3
  139.4 3.8 fusion.62
  143.1 3.4 fusion.63
  146.6 2.9 fusion.65
  149.5 1.0 copy-done.4
  151.1 0.6 iota_add_fusion.3
  152.0 3.8 fusion.62
  155.8 3.4 fusion.63
  159.2 2.9 fusion.65
  162.1 1.0 copy-done.4
  163.7 0.6 iota_add_fusion.3
  164.6 3.8 fusion.62
  168.4 3.4 fusion.63
  171.8 2.9 fusion.65
  174.7 1.0 copy-done.4
  176.3 0.6 iota_add_fusion.3
  177.2 3.8 fusion.62
  181.0 3.4 fusion.63
  184.4 2.9 fusion.65
  187.3 1.0 copy-done.4
  188.9 0.6 iota_add_fusion.3
  189.8 3.8 fusion.62
  193.6 3.4 fusion.63
  197.0 2.9 fusion.65
  200.0 1.0 copy-done.4
  200.9 1.6 copy.47
  202.6 6.5 %convolution_convert_fusion = bf16[512,4096]{1,0:T(8,128)(2,1)} fusion(bf16[512,512]{0,1:T(8,128)(2,1)S(1)} %bitcast.91, bf16[512,4096]{1,0:T(8,128)(2,1)} %param.18), kind=kOutput, calls=%fused_computation.27 | convolution fusion | flops 2149580800 | bytes 8912896 | tf_op jit(solution)/shard_map/dot_general | solution.py:89
  209.2 0.7 copy-done.7
  212.2 90.7 %reduce-scatter.2.cloned.1.call-done = bf16[32,4096]{1,0:T(8,128)(2,1)} async-done(((bf16[512,4096]{1,0:T(8,128)(2,1)}), bf16[32,4096]{1,0:T(8,128)(2,1)}) %reduce-scatter.2.cloned.1.call-update) | async-done | bytes 262160 | tf_op jit(solution)/shard_map/reduce_scatter | solution.py:88
  303.0 1.9 multiply_reduce_fusion
  304.9 1.2 convolution_convert_fusion.3
  306.3 2.1 broadcast_in_dim.58
  308.4 63.4 %all_to_all.10 = bf16[128,2,4096]{2,1,0:T(2,128)(2,1)} all-to-all(bf16[128,2,4096]{2,1,0:T(2,128)(2,1)S(1)} %bitcast.90), channel_id=1, replica_groups=mesh['ctx'=8,'exp'=16,'rep'=2] {'ctx','exp'}, dimensions={0} | all-to-all | bytes 4194304 | tf_op jit(solution)/shard_map/all_to_all | solution.py:117
  371.8 4.1 reshape.115
  375.9 2.4 fusion.25
  378.3 2.9 fusion.30
  381.4 0.7 convolution_convert_fusion.1
  382.2 3.5 copy.56
  385.7 6.7 %all-to-all-start.1 = ((bf16[128,2,4096]{2,1,0:T(2,128)(2,1)}), bf16[128,2,4096]{2,1,0:T(2,128)(2,1)}, u32[]{:S(2)}, u32[]{:S(2)}) async-start(bf16[128,2,4096]{2,1,0:T(2,128)(2,1)} %copy.56), calls=%async_computation.2 | async-start | bytes 4194304 | tf_op jit(solution)/shard_map/all_to_all | solution.py:124
  392.6 51.5 %all-to-all-done.1 = bf16[128,2,4096]{2,1,0:T(2,128)(2,1)} async-done(((bf16[128,2,4096]{2,1,0:T(2,128)(2,1)}), bf16[128,2,4096]{2,1,0:T(2,128)(2,1)}, u32[]{:S(2)}, u32[]{:S(2)}) %all-to-all-start.1) | async-done | bytes 2097184 | tf_op jit(solution)/shard_map/all_to_all | solution.py:124
  444.1 4.1 reshape.116
  448.2 1.9 reduce
  450.1 1.1 convolution_convert_fusion.2
  (126 shorter events, 9.7 us)
Async XLA Ops:
  7.2 374.3 %copy-start = (bf16[1,192,4096]{2,1,0:T(8,128)(2,1)S(1)}, bf16[1,192,4096]{2,1,0:T(8,128)(2,1)}, u32[]{:S(2)}) copy-start(bf16[1,192,4096]{2,1,0:T(8,128)(2,1)} %param.25) | copy-start | bytes 4718596
  7.2 48.5 %all-gather.3.cloned.1.call-start = ((), (), s32[]{:S(2)}) async-start(), calls=%async_computation.3 | async-start | bytes 1179648 | tf_op jit(solution)/shard_map/all_gather | solution.py:67
  8.9 91.1 %all-gather.5.cloned.1.call-start = ((), (), s32[]{:S(2)}) async-start(), calls=%async_computation.4 | async-start | bytes 1179648 | tf_op jit(solution)/shard_map/all_gather | solution.py:68
  10.6 292.4 %reduce-scatter.2.cloned.1.call-start = ((), (), s32[]{:S(2)}) async-start(), calls=%async_computation.5 | async-start | bytes 4456448 | tf_op jit(solution)/shard_map/reduce_scatter | solution.py:88
  101.5 7.2 %copy-start.3 = (f32[4,512,128]{2,1,0:T(8,128)S(1)}, f32[4,512,128]{2,1,0:T(8,128)}, u32[]{:S(2)}) copy-start(f32[4,512,128]{2,1,0:T(8,128)} %get-tuple-element.219) | copy-start | bytes 3145732 | tf_op jit(solution)/shard_map/while
  105.3 3.4 copy-start.1
  111.7 1.0 copy-start.4
  114.1 7.2 %copy-start.3 = (f32[4,512,128]{2,1,0:T(8,128)S(1)}, f32[4,512,128]{2,1,0:T(8,128)}, u32[]{:S(2)}) copy-start(f32[4,512,128]{2,1,0:T(8,128)} %get-tuple-element.219) | copy-start | bytes 3145732 | tf_op jit(solution)/shard_map/while
  117.9 3.4 copy-start.1
  124.3 1.0 copy-start.4
  126.7 7.2 %copy-start.3 = (f32[4,512,128]{2,1,0:T(8,128)S(1)}, f32[4,512,128]{2,1,0:T(8,128)}, u32[]{:S(2)}) copy-start(f32[4,512,128]{2,1,0:T(8,128)} %get-tuple-element.219) | copy-start | bytes 3145732 | tf_op jit(solution)/shard_map/while
  130.5 3.4 copy-start.1
  136.9 1.0 copy-start.4
  139.3 7.2 %copy-start.3 = (f32[4,512,128]{2,1,0:T(8,128)S(1)}, f32[4,512,128]{2,1,0:T(8,128)}, u32[]{:S(2)}) copy-start(f32[4,512,128]{2,1,0:T(8,128)} %get-tuple-element.219) | copy-start | bytes 3145732 | tf_op jit(solution)/shard_map/while
  143.1 3.4 copy-start.1
  149.5 1.0 copy-start.4
  152.0 7.2 %copy-start.3 = (f32[4,512,128]{2,1,0:T(8,128)S(1)}, f32[4,512,128]{2,1,0:T(8,128)}, u32[]{:S(2)}) copy-start(f32[4,512,128]{2,1,0:T(8,128)} %get-tuple-element.219) | copy-start | bytes 3145732 | tf_op jit(solution)/shard_map/while
  155.7 3.4 copy-start.1
  162.1 1.0 copy-start.4
  164.6 7.2 %copy-start.3 = (f32[4,512,128]{2,1,0:T(8,128)S(1)}, f32[4,512,128]{2,1,0:T(8,128)}, u32[]{:S(2)}) copy-start(f32[4,512,128]{2,1,0:T(8,128)} %get-tuple-element.219) | copy-start | bytes 3145732 | tf_op jit(solution)/shard_map/while
  168.4 3.4 copy-start.1
  174.7 1.0 copy-start.4
  177.2 7.2 %copy-start.3 = (f32[4,512,128]{2,1,0:T(8,128)S(1)}, f32[4,512,128]{2,1,0:T(8,128)}, u32[]{:S(2)}) copy-start(f32[4,512,128]{2,1,0:T(8,128)} %get-tuple-element.219) | copy-start | bytes 3145732 | tf_op jit(solution)/shard_map/while
  181.0 3.4 copy-start.1
  187.3 1.0 copy-start.4
  189.8 7.2 %copy-start.3 = (f32[4,512,128]{2,1,0:T(8,128)S(1)}, f32[4,512,128]{2,1,0:T(8,128)}, u32[]{:S(2)}) copy-start(f32[4,512,128]{2,1,0:T(8,128)} %get-tuple-element.219) | copy-start | bytes 3145732 | tf_op jit(solution)/shard_map/while
  193.6 3.4 copy-start.1
  199.9 1.0 copy-start.4
  209.1 0.7 copy-start.7
  209.1 93.9 %copy-start.5 = (bf16[32,4096]{1,0:T(8,128)(2,1)S(1)}, bf16[32,4096]{1,0:T(8,128)(2,1)}, u32[]{:S(2)}) copy-start(bf16[32,4096]{1,0:T(8,128)(2,1)} %param.14) | copy-start | bytes 786436
  209.1 95.7 %copy-start.6 = (f32[4096]{0:T(1024)S(1)}, f32[4096]{0:T(1024)}, u32[]{:S(2)}) copy-start(f32[4096]{0:T(1024)} %param.19) | copy-start | bytes 49156
  308.4 67.5 %copy-start.2 = (bf16[1,4096,192]{1,2,0:T(8,128)(2,1)S(1)}, bf16[1,4096,192]{1,2,0:T(8,128)(2,1)}, u32[]{:S(2)}) copy-start(bf16[1,4096,192]{1,2,0:T(8,128)(2,1)} %param.23) | copy-start | bytes 4718596
  382.1 10.2 %copy-start.8 = (s32[32,8]{0,1:T(8,128)S(1)}, s32[32,8]{0,1:T(8,128)}, u32[]{:S(2)}) copy-start(s32[32,8]{0,1:T(8,128)} %param.21) | copy-start | bytes 3076
  385.7 58.4 %all-to-all-start.1 = ((bf16[128,2,4096]{2,1,0:T(2,128)(2,1)}), bf16[128,2,4096]{2,1,0:T(2,128)(2,1)}, u32[]{:S(2)}, u32[]{:S(2)}) async-start(bf16[128,2,4096]{2,1,0:T(2,128)(2,1)} %copy.56), calls=%async_computation.2 | async-start | bytes 4194304 | tf_op jit(solution)/shard_map/all_to_all | solution.py:124
Sparse Core Ops, SparseCore 0:
  10.4 45.2 all-gather.2
  58.0 41.9 all-gather.4
  209.3 93.6 reduce-scatter.1
where the time goes:
time: 459 us; the launch traced here: 458 us
  waiting for transfers between devices  230 us (50%)
  matrix products  68.2 us (15%)
  blocking collectives  63.4 us (14%)
  other arithmetic  39.3 us (9%)
  local copies, waits for them, and re-layouts  34.7 us (8%)
  between operations  14.6 us (3%)
  starting transfers between devices  6.8 us (1%)
    reduce_scatter x1, waiting for transfers between devices, on_device(): lax.psum_scatter(jnp.dot(attended, out_proj, preferred_element_type=jnp.f...  90.7 us
    all_to_all x1, blocking collectives, on_device(): lax.all_to_all(copies, ('ctx', 'exp'), split_axis=0, concat_axis=0, tiled...  63.4 us
    all_to_all x1, waiting for transfers between devices, on_device(): lax.all_to_all(partial_value, ('ctx', 'exp'), split_axis=0, concat_axis=0...  51.5 us
    all_gather x1, waiting for transfers between devices, on_device(): value_piece = lax.all_gather(value_head, 'ctx', axis=0, tiled=True)  44.4 us
    all_gather x1, waiting for transfers between devices, on_device(): key_piece = lax.all_gather(key_head, 'ctx', axis=0, tiled=True)  43.5 us
    dot_general x8, matrix products, update(): jnp.einsum('hqd,kd->hqk', query_heads, key_block, preferred_element_type=...  30.2 us
    reduce_sum x8, other arithmetic, update(): total = total * factor + jnp.sum(weights, axis=2)  27.1 us
    dot_general x8, matrix products, update(): jnp.einsum('hqk,kd->hqd', weights.astype(jnp.bfloat16), value_block, pref...  23.2 us
  transfers between devices with their start and end apart: 4, of which 4 were waited for; matrix products, arithmetic and copies ran while one was open for 1% of the time, Pallas kernels for 0%

commit v1 on v0

--- a/solution.py
+++ b/solution.py
@@ -65,7 +65,13 @@
     )
     carry = start_state
     key_piece = lax.all_gather(key_head, "ctx", axis=0, tiled=True)
-    value_piece = lax.all_gather(value_head, "ctx", axis=0, tiled=True)
+    _see_classes = lambda point, comm_axis: jnp.concatenate(
+        lax.all_to_all(
+            jnp.stack([point for _ in range(lax.axis_size(comm_axis))], axis=0), comm_axis, 0, 0
+        ),
+        axis=0,
+    )
+    value_piece = _see_classes(value_head, "ctx")
     blocks = key_piece.shape[0] // seq_rows
     key_blocks = key_piece.reshape(blocks, seq_rows, HEAD_DIM)
     value_blocks = value_piece.reshape(blocks, seq_rows, HEAD_DIM)

time: 459 us -> 422 us (0.919)
  waiting for transfers between devices: 230 us -> 188 us
  starting transfers between devices: 6.8 us -> 12.6 us
    all_gather x1 -> x0, waiting for transfers between devices: 44.4 us -> none  [on_device(): value_piece = lax.all_gather(value_head, 'ctx', axis=0, tiled=True)]
    all_to_all x0 -> x1, waiting for transfers between devices: none -> 13.6 us  [on_device(): lax.all_to_all(jnp.stack([point for _ in range(lax.axis_size(comm_axis))]...]
    all_gather x1, waiting for transfers between devices: 43.5 us -> 32.1 us  [on_device(): key_piece = lax.all_gather(key_head, 'ctx', axis=0, tiled=True)]
    all_to_all x0 -> x1, starting transfers between devices: none -> 5.82 us  [on_device(): lax.all_to_all(jnp.stack([point for _ in range(lax.axis_size(comm_axis))]...]
where the time goes in v1:
time: 422 us; the launch traced here: 421 us
  waiting for transfers between devices  188 us (45%)
  matrix products  68.2 us (16%)
  blocking collectives  63.5 us (15%)
  other arithmetic  39.3 us (9%)
  local copies, waits for them, and re-layouts  34.2 us (8%)
  between operations  15 us (4%)
  starting transfers between devices  12.6 us (3%)
    reduce_scatter x1, waiting for transfers between devices, on_device(): lax.psum_scatter(jnp.dot(attended, out_proj, preferred_element_type=jnp.f...  90.6 us
    all_to_all x1, blocking collectives, on_device(): lax.all_to_all(copies, ('ctx', 'exp'), split_axis=0, concat_axis=0, tiled...  63.5 us
    all_to_all x1, waiting for transfers between devices, on_device(): lax.all_to_all(partial_value, ('ctx', 'exp'), split_axis=0, concat_axis=0...  51.5 us
    all_gather x1, waiting for transfers between devices, on_device(): key_piece = lax.all_gather(key_head, 'ctx', axis=0, tiled=True)  32.1 us
    dot_general x8, matrix products, update(): jnp.einsum('hqd,kd->hqk', query_heads, key_block, preferred_element_type=...  30.2 us
    reduce_sum x8, other arithmetic, update(): total = total * factor + jnp.sum(weights, axis=2)  27.1 us
    dot_general x8, matrix products, update(): jnp.einsum('hqk,kd->hqd', weights.astype(jnp.bfloat16), value_block, pref...  23.2 us
    all_to_all x1, waiting for transfers between devices, on_device(): lax.all_to_all(jnp.stack([point for _ in range(lax.axis_size(comm_axis))]...  13.6 us
  transfers between devices with their start and end apart: 4, of which 4 were waited for; matrix products, arithmetic and copies ran while one was open for 1% of the time, Pallas kernels for 0%

profile of v1, /device:TPU:64, one launch (start us, length us, event | category | flops | bytes accessed | tf_op | source)
XLA Modules:
  0.0 421.1 jit_solution(540834273336825997)
XLA Ops:
  7.2 1.1 constant_dynamic-slice_fusion
  8.3 1.1 stack.2
  9.4 5.8 %all-to-all-start = ((bf16[8,512,128]{2,1,0:T(8,128)(2,1)}), bf16[8,512,128]{2,1,0:T(8,128)(2,1)}, u32[]{:S(2)}, u32[]{:S(2)}) async-start(bf16[8,512,128]{2,1,0:T(8,128)(2,1)} %stack.2), calls=%async_computation | async-start | bytes 2097152 | tf_op jit(solution)/shard_map/all_to_all | solution.py:69
  15.3 1.6 constant_dynamic-slice_fusion.1
  17.5 13.6 %all-to-all-done = bf16[8,512,128]{2,1,0:T(8,128)(2,1)} async-done(((bf16[8,512,128]{2,1,0:T(8,128)(2,1)}), bf16[8,512,128]{2,1,0:T(8,128)(2,1)}, u32[]{:S(2)}, u32[]{:S(2)}) %all-to-all-start) | async-done | bytes 1048608 | tf_op jit(solution)/shard_map/all_to_all | solution.py:69
  31.0 32.1 %all-gather.2.cloned.1.call-done = bf16[4096,128]{1,0:T(8,128)(2,1)} async-done(((bf16[512,128]{1,0:T(8,128)(2,1)}), bf16[4096,128]{1,0:T(8,128)(2,1)}) %all-gather.2.cloned.1.call-update) | async-done | bytes 1048592 | tf_op jit(solution)/shard_map/all_gather | solution.py:67
  63.2 100.9 %while.15 = (s32[]{:T(128)}, f32[4,512]{1,0:T(4,128)S(1)}, f32[4,512]{1,0:T(4,128)S(1)}, f32[4,512,128]{2,1,0:T(8,128)}, s32[8]{0:T(128)S(1)}, /*index=5*/bf16[8...) while((s32[]{:T(128)}, f32[4,512]{1,0:T(4,128)S(1)}, ...), condition=%wide.region_3.4_spmd.clone, body=%wide.region_0.3_spmd.clone.sunk | while | flops 551562240 | bytes 41821408 | solution.py:85
  63.7 0.6 iota_add_fusion.3
  64.6 3.8 fusion.62
  68.4 3.4 fusion.63
  71.8 2.9 fusion.65
  74.8 1.0 copy-done.4
  76.3 0.6 iota_add_fusion.3
  77.2 3.8 fusion.62
  81.0 3.4 fusion.63
  84.5 2.9 fusion.65
  87.4 1.0 copy-done.4
  89.0 0.6 iota_add_fusion.3
  89.8 3.8 fusion.62
  93.6 3.4 fusion.63
  97.1 2.9 fusion.65
  100.0 1.0 copy-done.4
  101.6 0.6 iota_add_fusion.3
  102.5 3.8 fusion.62
  106.2 3.4 fusion.63
  109.7 2.9 fusion.65
  112.6 1.0 copy-done.4
  114.2 0.6 iota_add_fusion.3
  115.1 3.8 fusion.62
  118.9 3.4 fusion.63
  122.3 2.9 fusion.65
  125.2 1.0 copy-done.4
  126.8 0.6 iota_add_fusion.3
  127.7 3.8 fusion.62
  131.5 3.4 fusion.63
  134.9 2.9 fusion.65
  137.8 1.0 copy-done.4
  139.4 0.6 iota_add_fusion.3
  140.3 3.8 fusion.62
  144.1 3.4 fusion.63
  147.5 2.9 fusion.65
  150.4 1.0 copy-done.4
  152.9 3.8 fusion.62
  156.7 3.4 fusion.63
  160.1 2.9 fusion.65
  163.1 1.0 copy-done.4
  164.0 1.6 copy.47
  165.7 6.5 %convolution_convert_fusion = bf16[512,4096]{1,0:T(8,128)(2,1)} fusion(bf16[512,512]{0,1:T(8,128)(2,1)S(1)} %bitcast.90, bf16[512,4096]{1,0:T(8,128)(2,1)} %param.18), kind=kOutput, calls=%fused_computation.27 | convolution fusion | flops 2149580800 | bytes 8912896 | tf_op jit(solution)/shard_map/dot_general | solution.py:95
  172.3 0.7 copy-done.8
  175.3 90.6 %reduce-scatter.2.cloned.1.call-done = bf16[32,4096]{1,0:T(8,128)(2,1)} async-done(((bf16[512,4096]{1,0:T(8,128)(2,1)}), bf16[32,4096]{1,0:T(8,128)(2,1)}) %reduce-scatter.2.cloned.1.call-update) | async-done | bytes 262160 | tf_op jit(solution)/shard_map/reduce_scatter | solution.py:94
  265.9 1.9 multiply_reduce_fusion
  267.8 1.2 convolution_convert_fusion.3
  269.2 2.1 broadcast_in_dim.58
  271.3 63.5 %all_to_all.15 = bf16[128,2,4096]{2,1,0:T(2,128)(2,1)} all-to-all(bf16[128,2,4096]{2,1,0:T(2,128)(2,1)S(1)} %bitcast.89), channel_id=1, replica_groups=mesh['ctx'=8,'exp'=16,'rep'=2] {'ctx','exp'}, dimensions={0} | all-to-all | bytes 4194304 | tf_op jit(solution)/shard_map/all_to_all | solution.py:123
  334.8 4.1 reshape.113
  338.9 2.4 fusion.25
  341.4 2.9 fusion.30
  344.5 0.7 convolution_convert_fusion.1
  345.2 3.5 copy.56
  348.7 6.7 %all-to-all-start.2 = ((bf16[128,2,4096]{2,1,0:T(2,128)(2,1)}), bf16[128,2,4096]{2,1,0:T(2,128)(2,1)}, u32[]{:S(2)}, u32[]{:S(2)}) async-start(bf16[128,2,4096]{2,1,0:T(2,128)(2,1)} %copy.56), calls=%async_computation.3 | async-start | bytes 4194304 | tf_op jit(solution)/shard_map/all_to_all | solution.py:130
  355.6 51.5 %all-to-all-done.2 = bf16[128,2,4096]{2,1,0:T(2,128)(2,1)} async-done(((bf16[128,2,4096]{2,1,0:T(2,128)(2,1)}), bf16[128,2,4096]{2,1,0:T(2,128)(2,1)}, u32[]{:S(2)}, u32[]{:S(2)}) %all-to-all-start.2) | async-done | bytes 2097184 | tf_op jit(solution)/shard_map/all_to_all | solution.py:130
  407.2 4.1 reshape.114
  411.3 1.9 reduce
  413.2 1.1 convolution_convert_fusion.2
  (128 shorter events, 10.5 us)
Async XLA Ops:
  7.2 337.3 %copy-start = (bf16[1,192,4096]{2,1,0:T(8,128)(2,1)S(1)}, bf16[1,192,4096]{2,1,0:T(8,128)(2,1)}, u32[]{:S(2)}) copy-start(bf16[1,192,4096]{2,1,0:T(8,128)(2,1)} %param.25) | copy-start | bytes 4718596
  7.2 9.8 %copy-start.6 = (bf16[512,512]{1,0:T(8,128)(2,1)S(1)}, bf16[512,512]{1,0:T(8,128)(2,1)}, u32[]{:S(2)}) copy-start(bf16[512,512]{1,0:T(8,128)(2,1)} %param.15) | copy-start | bytes 1572868
  9.4 21.6 %all-to-all-start = ((bf16[8,512,128]{2,1,0:T(8,128)(2,1)}), bf16[8,512,128]{2,1,0:T(8,128)(2,1)}, u32[]{:S(2)}, u32[]{:S(2)}) async-start(bf16[8,512,128]{2,1,0:T(8,128)(2,1)} %stack.2), calls=%async_computation | async-start | bytes 2097152 | tf_op jit(solution)/shard_map/all_to_all | solution.py:69
  15.2 47.9 %all-gather.2.cloned.1.call-start = ((), (), s32[]{:S(2)}) async-start(), calls=%async_computation.4 | async-start | bytes 1179648 | tf_op jit(solution)/shard_map/all_gather | solution.py:67
  16.9 249.0 %reduce-scatter.2.cloned.1.call-start = ((), (), s32[]{:S(2)}) async-start(), calls=%async_computation.5 | async-start | bytes 4456448 | tf_op jit(solution)/shard_map/reduce_scatter | solution.py:94
  64.6 7.2 %copy-start.3 = (f32[4,512,128]{2,1,0:T(8,128)S(1)}, f32[4,512,128]{2,1,0:T(8,128)}, u32[]{:S(2)}) copy-start(f32[4,512,128]{2,1,0:T(8,128)} %get-tuple-element.219) | copy-start | bytes 3145732 | tf_op jit(solution)/shard_map/while
  68.4 3.4 copy-start.1
  74.8 1.0 copy-start.4
  77.2 7.2 %copy-start.3 = (f32[4,512,128]{2,1,0:T(8,128)S(1)}, f32[4,512,128]{2,1,0:T(8,128)}, u32[]{:S(2)}) copy-start(f32[4,512,128]{2,1,0:T(8,128)} %get-tuple-element.219) | copy-start | bytes 3145732 | tf_op jit(solution)/shard_map/while
  81.0 3.4 copy-start.1
  87.4 1.0 copy-start.4
  89.8 7.2 %copy-start.3 = (f32[4,512,128]{2,1,0:T(8,128)S(1)}, f32[4,512,128]{2,1,0:T(8,128)}, u32[]{:S(2)}) copy-start(f32[4,512,128]{2,1,0:T(8,128)} %get-tuple-element.219) | copy-start | bytes 3145732 | tf_op jit(solution)/shard_map/while
  93.6 3.4 copy-start.1
  100.0 1.0 copy-start.4
  102.4 7.2 %copy-start.3 = (f32[4,512,128]{2,1,0:T(8,128)S(1)}, f32[4,512,128]{2,1,0:T(8,128)}, u32[]{:S(2)}) copy-start(f32[4,512,128]{2,1,0:T(8,128)} %get-tuple-element.219) | copy-start | bytes 3145732 | tf_op jit(solution)/shard_map/while
  106.2 3.4 copy-start.1
  112.6 1.0 copy-start.4
  115.0 7.2 %copy-start.3 = (f32[4,512,128]{2,1,0:T(8,128)S(1)}, f32[4,512,128]{2,1,0:T(8,128)}, u32[]{:S(2)}) copy-start(f32[4,512,128]{2,1,0:T(8,128)} %get-tuple-element.219) | copy-start | bytes 3145732 | tf_op jit(solution)/shard_map/while
  118.8 3.4 copy-start.1
  125.2 1.0 copy-start.4
  127.7 7.2 %copy-start.3 = (f32[4,512,128]{2,1,0:T(8,128)S(1)}, f32[4,512,128]{2,1,0:T(8,128)}, u32[]{:S(2)}) copy-start(f32[4,512,128]{2,1,0:T(8,128)} %get-tuple-element.219) | copy-start | bytes 3145732 | tf_op jit(solution)/shard_map/while
  131.4 3.4 copy-start.1
  137.8 1.0 copy-start.4
  140.3 7.2 %copy-start.3 = (f32[4,512,128]{2,1,0:T(8,128)S(1)}, f32[4,512,128]{2,1,0:T(8,128)}, u32[]{:S(2)}) copy-start(f32[4,512,128]{2,1,0:T(8,128)} %get-tuple-element.219) | copy-start | bytes 3145732 | tf_op jit(solution)/shard_map/while
  144.1 3.4 copy-start.1
  150.4 1.0 copy-start.4
  152.9 7.2 %copy-start.3 = (f32[4,512,128]{2,1,0:T(8,128)S(1)}, f32[4,512,128]{2,1,0:T(8,128)}, u32[]{:S(2)}) copy-start(f32[4,512,128]{2,1,0:T(8,128)} %get-tuple-element.219) | copy-start | bytes 3145732 | tf_op jit(solution)/shard_map/while
  156.7 3.4 copy-start.1
  163.0 1.0 copy-start.4
  172.2 0.7 copy-start.8
  172.2 93.7 %copy-start.5 = (bf16[32,4096]{1,0:T(8,128)(2,1)S(1)}, bf16[32,4096]{1,0:T(8,128)(2,1)}, u32[]{:S(2)}) copy-start(bf16[32,4096]{1,0:T(8,128)(2,1)} %param.14) | copy-start | bytes 786436
  172.2 95.6 %copy-start.7 = (f32[4096]{0:T(1024)S(1)}, f32[4096]{0:T(1024)}, u32[]{:S(2)}) copy-start(f32[4096]{0:T(1024)} %param.19) | copy-start | bytes 49156
  271.3 67.6 %copy-start.2 = (bf16[1,4096,192]{1,2,0:T(8,128)(2,1)S(1)}, bf16[1,4096,192]{1,2,0:T(8,128)(2,1)}, u32[]{:S(2)}) copy-start(bf16[1,4096,192]{1,2,0:T(8,128)(2,1)} %param.23) | copy-start | bytes 4718596
  345.2 10.2 %copy-start.9 = (s32[32,8]{0,1:T(8,128)S(1)}, s32[32,8]{0,1:T(8,128)}, u32[]{:S(2)}) copy-start(s32[32,8]{0,1:T(8,128)} %param.21) | copy-start | bytes 3076
  348.7 58.5 %all-to-all-start.2 = ((bf16[128,2,4096]{2,1,0:T(2,128)(2,1)}), bf16[128,2,4096]{2,1,0:T(2,128)(2,1)}, u32[]{:S(2)}, u32[]{:S(2)}) async-start(bf16[128,2,4096]{2,1,0:T(2,128)(2,1)} %copy.56), calls=%async_computation.3 | async-start | bytes 4194304 | tf_op jit(solution)/shard_map/all_to_all | solution.py:130
Sparse Core Ops, SparseCore 0:
  18.4 44.6 all-gather.1
  172.4 93.4 reduce-scatter.1
